TPU v7x, 32 devices: a whole 2x2x4 slice. The times are simulated.
32 devices in a mesh: doc: 8 (over y, x, core), seq: 4 (over z).
Axes of the slice: x: 2, y: 2, z: 4, core: 2. Of those that a mesh axis runs over, the one named last changes fastest.
Arguments:
- images: bfloat16 [8, 4, 128, 8192], P('doc', None, None, 'seq'), may hold values from -6 to 6
- kv_weight: bfloat16 [1024, 8192], P('doc', 'seq'), may hold values from -0.0625 to 0.0625
- q_gain: float32 [128], replicated, may hold values from 0.1 to 1.9
- k_gain: float32 [128], replicated, may hold values from 0.1 to 1.9
- queries: bfloat16 [8, 512, 4096], P('doc', 'seq'), may hold values from -6 to 6
- cotangent: bfloat16 [8, 512, 4096], P('doc', 'seq'), may hold values from -6 to 6
- tile_count: int32 [8], replicated, may hold values from 1 to 4, as said below
- tile_target: int32 [8, 4], replicated, may hold values from 0 to 8, as said below
- tile_source: int32 [8, 4], replicated, may hold values from 0 to 8, as said below
- text_length: int32 [8], replicated, may hold values from 64 to 512, as said below
Outputs:
- attn_out: bfloat16 [8, 512, 4096], P('doc', 'seq')
- kv_weight_grad: float32 [1024, 8192], P('doc', 'seq')
Inputs may be any that keep to these rules, and one draw needn't show every extreme that they name: `tile_count`: some document has 4 tiles and some has 1. `tile_target`: 8 marks an empty slot. The tile in slot k of an encoder device is tile k of its document; no encoder device holds two tiles of one document. Agrees with tile_source and tile_count. `tile_source`: 8 for k at or beyond the document's tile count; otherwise the encoder device that holds tile k in its slot k. `text_length`: live rows come first; some document has all 512 rows live.
All inputs are finite; a program needn't handle non-finite values.
Results may differ from a plain program's by a relative error of at most 0.03.
Values may be sent and summed in bfloat16 or wider, within the bound.
No kernel may reach another device: no remote copies, remote signals or barrier semaphores. Data moves between devices by JAX's collectives and lax.ppermute only.
A program may use at most 64 MiB of HBM per device.

v0:
```python
import math
import jax
import jax.numpy as jnp
from jax import lax
from jax.sharding import PartitionSpec as P

EPS = 1e-05


def cross_core(kv_tiles, query_rows, grad_rows, q_gain, k_gain, key_live, row_live):
    key_width = kv_tiles.shape[-1] // 2
    head_dim = q_gain.shape[0]
    kv_heads = key_width // head_dim
    token_rows = query_rows.shape[0]
    q_heads = query_rows.shape[1] // head_dim
    group_size = q_heads // kv_heads
    inv_root = 1.0 / math.sqrt(head_dim)
    key_raw = kv_tiles[:, :key_width].reshape(-1, kv_heads, head_dim).astype(jnp.float32)
    values = kv_tiles[:, key_width:].reshape(-1, kv_heads, head_dim)
    key_scale = lax.rsqrt(jnp.mean(key_raw * key_raw, axis=-1, keepdims=True) + EPS)
    key_normed = (key_raw * key_scale * k_gain).astype(jnp.bfloat16)
    query_raw = query_rows.reshape(token_rows, kv_heads, group_size, head_dim).astype(jnp.float32)
    query_scale = lax.rsqrt(jnp.mean(query_raw * query_raw, axis=-1, keepdims=True) + EPS)
    query_normed = (query_raw * query_scale * q_gain).astype(jnp.bfloat16)
    row_mask = row_live[:, None, None, None]
    grad_live = grad_rows.reshape(token_rows, kv_heads, group_size, head_dim) * row_mask.astype(
        jnp.bfloat16
    )

    def one_head(items):
        key_head, value_head, query_head, grad_head = items
        scores = (
            jnp.einsum("tgd,ld->tgl", query_head, key_head, preferred_element_type=jnp.float32)
            * inv_root
        )
        expd = jnp.exp(scores) * key_live
        attend = expd / jnp.sum(expd, axis=-1, keepdims=True)
        attend_low = attend.astype(jnp.bfloat16)
        mixed = jnp.einsum(
            "tgl,ld->tgd", attend_low, value_head, preferred_element_type=jnp.float32
        )
        mixed_low = (mixed * row_live[:, None, None]).astype(jnp.bfloat16)
        grad_attend = jnp.einsum(
            "tgd,ld->tgl", grad_head, value_head, preferred_element_type=jnp.float32
        )
        grad_scores = attend * (grad_attend - jnp.sum(attend * grad_attend, axis=-1, keepdims=True))
        grad_low = (grad_scores * inv_root).astype(jnp.bfloat16)
        grad_keyn = jnp.einsum(
            "tgl,tgd->ld", grad_low, query_head, preferred_element_type=jnp.float32
        )
        grad_values = jnp.einsum(
            "tgl,tgd->ld", attend_low, grad_head, preferred_element_type=jnp.float32
        )
        return (mixed_low, grad_keyn, grad_values)

    head_items = (
        jnp.moveaxis(key_normed, 1, 0),
        jnp.moveaxis(values, 1, 0),
        jnp.moveaxis(query_normed, 1, 0),
        jnp.moveaxis(grad_live, 1, 0),
    )
    mixed_heads, keyn_heads, value_heads = lax.map(one_head, head_items)
    attn_rows = jnp.moveaxis(mixed_heads, 0, 1).reshape(token_rows, -1)
    grad_keyn = jnp.moveaxis(keyn_heads, 0, 1)
    grad_values = jnp.moveaxis(value_heads, 0, 1)
    weighted = grad_keyn * k_gain
    cubed = key_scale * key_scale * key_scale
    grad_keys = key_scale * weighted - key_raw * cubed * jnp.mean(
        weighted * key_raw, axis=-1, keepdims=True
    )
    grad_kv = jnp.concatenate(
        [grad_keys.reshape(-1, key_width), grad_values.reshape(-1, key_width)], axis=-1
    )
    return (attn_rows, grad_kv)


def per_device(
    images,
    kv_weight,
    q_gain,
    k_gain,
    queries,
    cotangent,
    tile_count,
    tile_target,
    tile_source,
    text_length,
):
    n_doc = lax.axis_size("doc")
    n_seq = lax.axis_size("seq")
    doc_at = lax.axis_index("doc")
    seq_at = lax.axis_index("seq")
    slots = images.shape[1]
    tile_rows = images.shape[2]
    part_rows = tile_rows // n_seq
    own_cols = images[0].reshape(slots * tile_rows, images.shape[3])
    partial_value = lax.dot_general(
        own_cols,
        lax.all_gather(kv_weight, "doc", axis=0, tiled=True),
        (((1,), (1,)), ((), ())),
        preferred_element_type=jnp.float32,
    )
    width = partial_value.shape[1]
    partial_value = partial_value.reshape(slots, tile_rows, width)
    summed = lax.psum(partial_value.astype(jnp.bfloat16), "seq").astype(jnp.float32)
    own_share = lax.dynamic_slice_in_dim(summed, seq_at * part_rows, part_rows, 1)
    kv_own = own_share.astype(jnp.bfloat16)
    doc_ids = jnp.arange(n_doc, dtype=jnp.int32)
    slot_ids = jnp.arange(slots, dtype=jnp.int32)
    targets = tile_target[doc_at]
    send_map = (targets[None, :] == doc_ids[:, None]).astype(jnp.bfloat16)
    outgoing = jnp.einsum(
        "ds,src->drc", send_map, kv_own, preferred_element_type=jnp.float32
    ).astype(jnp.bfloat16)
    incoming = lax.all_to_all(outgoing, "doc", split_axis=0, concat_axis=0, tiled=True)
    tiles_here = tile_count[doc_at]
    sources = tile_source[doc_at]
    live_slot = slot_ids < tiles_here
    pick_map = ((sources[:, None] == doc_ids[None, :]) & live_slot[:, None]).astype(jnp.bfloat16)
    kv_part = jnp.einsum(
        "se,erc->src", pick_map, incoming, preferred_element_type=jnp.float32
    ).astype(jnp.bfloat16)
    kv_full = lax.all_gather(kv_part, "seq", axis=1, tiled=True)
    token_rows = queries.shape[1]
    key_live = (jnp.arange(slots * tile_rows, dtype=jnp.int32) // tile_rows < tiles_here).astype(
        jnp.float32
    )
    row_index = seq_at * token_rows + jnp.arange(token_rows, dtype=jnp.int32)
    row_live = (row_index < text_length[doc_at]).astype(jnp.float32)
    attn_rows, grad_kv = cross_core(
        kv_full.reshape(slots * tile_rows, width),
        queries[0],
        cotangent[0],
        q_gain,
        k_gain,
        key_live,
        row_live,
    )
    attn_out = attn_rows[None]
    grad_kv = grad_kv.reshape(slots, tile_rows, width)
    grad_sum = lax.psum(grad_kv.astype(jnp.bfloat16), "seq").astype(jnp.float32)
    grad_share = lax.dynamic_slice_in_dim(grad_sum, seq_at * part_rows, part_rows, 1)
    grad_own = grad_share.astype(jnp.bfloat16)
    back_out = jnp.einsum(
        "se,src->erc", pick_map, grad_own, preferred_element_type=jnp.float32
    ).astype(jnp.bfloat16)
    back_in = lax.all_to_all(back_out, "doc", split_axis=0, concat_axis=0, tiled=True)
    returned = jnp.einsum(
        "ds,drc->src", send_map, back_in, preferred_element_type=jnp.float32
    ).astype(jnp.bfloat16)
    grad_full = lax.all_gather(returned, "seq", axis=1, tiled=True)
    grad_flat = grad_full.reshape(slots * tile_rows, width)
    rows_each = width // n_doc
    weight_part = lax.dot_general(
        grad_flat, own_cols, (((0,), (0,)), ((), ())), preferred_element_type=jnp.float32
    )
    weight_sum = lax.psum(weight_part.astype(jnp.bfloat16), "doc").astype(jnp.float32)
    weight_grad = lax.dynamic_slice_in_dim(weight_sum, doc_at * rows_each, rows_each, 0)
    return (attn_out, weight_grad)


def solution(mesh):
    return jax.shard_map(
        per_device,
        mesh=mesh,
        in_specs=(
            P("doc", None, None, "seq"),
            P("doc", "seq"),
            P(),
            P(),
            P("doc", "seq", None),
            P("doc", "seq", None),
            P(),
            P(),
            P(),
            P(),
        ),
        out_specs=(P("doc", "seq", None), P("doc", "seq")),
        check_vma=False,
    )
```

profile of v0, /device:TPU:0, one launch (start us, length us, event | category | flops | bytes accessed | tf_op | source)
XLA Modules:
  0.0 441.7 jit_solution(6251067855293527332)
XLA Ops:
  8.0 41.2 %all-gather.4.cloned.1.call-done = bf16[1024,2048]{1,0:T(8,128)(2,1)} async-done(((bf16[128,2048]{1,0:T(8,128)(2,1)}), bf16[1024,2048]{1,0:T(8,128)(2,1)}) %all-gather.4.cloned.1.call-update) | async-done | bytes 4194320 | tf_op jit(solution)/shard_map/all_gather | solution.py:99
  49.2 5.5 %fusion.64 = bf16[4,128,1024]{2,1,0:T(8,128)(2,1)} fusion(bf16[1024,2048]{1,0:T(8,128)(2,1)} %all-gather.4.cloned.1.call-done, bf16[1,4,128,2048]{3,2,1,0:T(8,128)(2,1)S(1)} %copy-done), kind=kOutput, calls=%fused_computation.63 | convolution fusion | flops 2148007936 | bytes 7340032 | tf_op jit(solution)/shard_map/dot_general | solution.py:97
  55.0 51.8 %all-reduce.4.cloned.1.call-done = bf16[4,128,1024]{2,1,0:T(8,128)(2,1)} async-done(((bf16[4,128,1024]{2,1,0:T(8,128)(2,1)}), bf16[4,128,1024]{2,1,0:T(8,128)(2,1)}) %all-reduce.4.cloned.1.call-update) | async-done | bytes 1048592 | tf_op jit(solution)/shard_map/psum | solution.py:105
  109.3 3.7 all-to-all-start
  114.5 8.2 %all-to-all-done = bf16[8,32,1024]{2,1,0:T(8,128)(2,1)S(1)} async-done(((bf16[8,32,1024]{2,1,0:T(8,128)(2,1)}), bf16[8,32,1024]{2,1,0:T(8,128)(2,1)S(1)}, u32[]{:S(2)}, u32[]{:S(2)}) %all-to-all-start) | async-done | bytes 524320 | tf_op jit(solution)/shard_map/all_to_all | solution.py:115
  124.8 2.3 copy.40
  127.0 1.6 copy.33
  129.6 2.3 multiply_bitcast_fusion
  131.9 1.4 fusion.69
  133.3 16.2 %all-gather.6.cloned.1.call-done = bf16[4,128,1024]{2,0,1:T(4,128)(2,1)} async-done(((bf16[4,32,1024]{2,0,1:T(4,128)(2,1)}), bf16[4,128,1024]{2,0,1:T(4,128)(2,1)}) %all-gather.6.cloned.1.call-update) | async-done | bytes 1048592 | tf_op jit(solution)/shard_map/all_gather | solution.py:123
  149.5 1.5 copy.37
  151.0 1.3 fusion.89
  152.3 1.6 copy.38
  154.0 2.1 copy.39
  157.1 87.8 %while.15 = (s32[]{:T(128)}, bf16[4,128,8,128]{3,1,2,0:T(8,128)(2,1)}, f32[4,512,128]{1,2,0:T(8,128)}, bf16[4,512,128]{2,1,0:T(8,128)(2,1)}, bf16[4,128,8,128]{1...) while((s32[]{:T(128)}, ...), condition=%wide.region_6.7_spmd.clone, body=%wide.region_3.6_spmd.clone.sunk | while | flops 682891136 | bytes 27433116 | solution.py:62
  157.7 2.8 fusion.115
  160.5 2.7 fusion.117
  163.2 9.8 %fusion.118 = f32[4,512,128]{1,2,0:T(8,128)} fusion(f32[4,512,128]{1,2,0:T(8,128)} %get-tuple-element.222, s32[]{:T(128)} %get-tuple-element.220, f32[128,8,512]{2,0,1:T(8,128)} %fusion.117, bf16[4,128,8,128]{1,3,2,0:T(8,128)(2,1)} %get-tuple-element.236, f32[128,8,512]{2,0,1:T(8,128)} %get-tuple-element.206, f32[128,8]{0,1:T(8,128)S(1)} %get-tuple-element.207, ...), kind=kOutput, calls=%fused_computation.13.clone.1 | convolution fusion | flops 139986432 | bytes 8926208 | tf_op jit(solution)/shard_map/while/body/eval_jaxpr/tgl,tgd->ld/dot_general | solution.py:48
  173.0 3.1 fusion.119
  176.8 2.2 fusion.116
  179.6 2.8 fusion.115
  182.4 2.7 fusion.117
  185.2 9.8 %fusion.118 = f32[4,512,128]{1,2,0:T(8,128)} fusion(f32[4,512,128]{1,2,0:T(8,128)} %get-tuple-element.222, s32[]{:T(128)} %get-tuple-element.220, f32[128,8,512]{2,0,1:T(8,128)} %fusion.117, bf16[4,128,8,128]{1,3,2,0:T(8,128)(2,1)} %get-tuple-element.236, f32[128,8,512]{2,0,1:T(8,128)} %get-tuple-element.206, f32[128,8]{0,1:T(8,128)S(1)} %get-tuple-element.207, ...), kind=kOutput, calls=%fused_computation.13.clone.1 | convolution fusion | flops 139986432 | bytes 8926208 | tf_op jit(solution)/shard_map/while/body/eval_jaxpr/tgl,tgd->ld/dot_general | solution.py:48
  195.0 3.1 fusion.119
  198.7 2.2 fusion.116
  201.6 2.8 fusion.115
  204.4 2.7 fusion.117
  207.1 9.8 %fusion.118 = f32[4,512,128]{1,2,0:T(8,128)} fusion(f32[4,512,128]{1,2,0:T(8,128)} %get-tuple-element.222, s32[]{:T(128)} %get-tuple-element.220, f32[128,8,512]{2,0,1:T(8,128)} %fusion.117, bf16[4,128,8,128]{1,3,2,0:T(8,128)(2,1)} %get-tuple-element.236, f32[128,8,512]{2,0,1:T(8,128)} %get-tuple-element.206, f32[128,8]{0,1:T(8,128)S(1)} %get-tuple-element.207, ...), kind=kOutput, calls=%fused_computation.13.clone.1 | convolution fusion | flops 139986432 | bytes 8926208 | tf_op jit(solution)/shard_map/while/body/eval_jaxpr/tgl,tgd->ld/dot_general | solution.py:48
  216.9 3.1 fusion.119
  220.7 2.2 fusion.116
  223.5 2.8 fusion.115
  226.3 2.7 fusion.117
  229.0 9.8 %fusion.118 = f32[4,512,128]{1,2,0:T(8,128)} fusion(f32[4,512,128]{1,2,0:T(8,128)} %get-tuple-element.222, s32[]{:T(128)} %get-tuple-element.220, f32[128,8,512]{2,0,1:T(8,128)} %fusion.117, bf16[4,128,8,128]{1,3,2,0:T(8,128)(2,1)} %get-tuple-element.236, f32[128,8,512]{2,0,1:T(8,128)} %get-tuple-element.206, f32[128,8]{0,1:T(8,128)S(1)} %get-tuple-element.207, ...), kind=kOutput, calls=%fused_computation.13.clone.1 | convolution fusion | flops 139986432 | bytes 8926208 | tf_op jit(solution)/shard_map/while/body/eval_jaxpr/tgl,tgd->ld/dot_general | solution.py:48
  238.9 3.1 fusion.119
  242.6 2.2 fusion.116
  244.8 1.5 fusion.72
  247.5 1.2 reshape.87
  250.9 2.5 pad_maximum_fusion
  253.5 51.4 %all-reduce.6.cloned.1.call-done = bf16[4,128,1024]{2,0,1:T(4,128)(2,1)} async-done(((bf16[4,128,1024]{2,0,1:T(4,128)(2,1)}), bf16[4,128,1024]{2,0,1:T(4,128)(2,1)}) %all-reduce.6.cloned.1.call-update) | async-done | bytes 1048592 | tf_op jit(solution)/shard_map/psum | solution.py:141
  304.9 1.4 convolution_convert_fusion.1
  306.5 13.2 %all_to_all.10 = bf16[8,32,1024]{2,1,0:T(8,128)(2,1)S(1)} all-to-all(bf16[8,32,1024]{2,1,0:T(8,128)(2,1)S(1)} %copy.51), channel_id=1, replica_groups=mesh['doc'=8,'seq'=4] {'doc'}, dimensions={0} | all-to-all | bytes 1048576 | tf_op jit(solution)/shard_map/all_to_all | solution.py:147
  321.1 25.3 %all-gather.8.cloned.1.call-done = bf16[4,128,1024]{2,0,1:T(4,128)(2,1)} async-done(((bf16[4,32,1024]{2,0,1:T(4,128)(2,1)}), bf16[4,128,1024]{2,0,1:T(4,128)(2,1)}) %all-gather.8.cloned.1.call-update) | async-done | bytes 1048592 | tf_op jit(solution)/shard_map/all_gather | solution.py:151
  346.5 1.5 copy.53
  348.0 4.4 convolution_convert_fusion
  352.4 1.9 copy.45
  354.3 1.3 broadcast_in_dim_reshape.3
  355.6 77.2 %all-reduce.8.cloned.1.call-done = bf16[1024,2048]{1,0:T(8,128)(2,1)} async-done(((bf16[1024,2048]{1,0:T(8,128)(2,1)}), bf16[1024,2048]{1,0:T(8,128)(2,1)}) %all-reduce.8.cloned.1.call-update) | async-done | bytes 4194320 | tf_op jit(solution)/shard_map/psum | solution.py:157
  432.7 2.1 dynamic-slice_convert_fusion
  (72 shorter events, 19.1 us)
Async XLA Ops:
  7.2 42.1 %copy-start = (bf16[1,4,128,2048]{3,2,1,0:T(8,128)(2,1)S(1)}, bf16[1,4,128,2048]{3,2,1,0:T(8,128)(2,1)}, u32[]{:S(2)}) copy-start(bf16[1,4,128,2048]{3,2,1,0:T(8,128)(2,1)} %param.12) | copy-start | bytes 6291460
  7.2 42.0 %all-gather.4.cloned.1.call-start = ((), (), s32[]{:S(2)}) async-start(), calls=%async_computation.2 | async-start | bytes 4718592 | tf_op jit(solution)/shard_map/all_gather | solution.py:99
  7.9 46.9 %copy-start.5 = (s32[8,4]{0,1:T(4,128)S(1)}, s32[8,4]{0,1:T(4,128)}, u32[]{:S(2)}) copy-start(s32[8,4]{0,1:T(4,128)} %param.19) | copy-start | bytes 388
  7.9 98.9 %all-reduce.4.cloned.1.call-start = ((), (), s32[]{:S(2)}) async-start(), calls=%async_computation.3 | async-start | bytes 2097152 | tf_op jit(solution)/shard_map/psum | solution.py:105
  54.7 58.3 %copy-start.8 = (s32[8]{0:T(128)S(1)}, s32[8]{0:T(128)}, u32[]{:S(2)}) copy-start(s32[8]{0:T(128)} %param.18) | copy-start | bytes 100
  54.7 58.9 %copy-start.6 = (s32[8,4]{0,1:T(4,128)S(1)}, s32[8,4]{0,1:T(4,128)}, u32[]{:S(2)}) copy-start(s32[8,4]{0,1:T(4,128)} %param.20) | copy-start | bytes 388
  107.8 16.3 %copy-start.9 = (s32[8]{0:T(128)S(1)}, s32[8]{0:T(128)}, u32[]{:S(2)}) copy-start(s32[8]{0:T(128)} %param.21) | copy-start | bytes 100
  109.3 13.4 %all-to-all-start = ((bf16[8,32,1024]{2,1,0:T(8,128)(2,1)}), bf16[8,32,1024]{2,1,0:T(8,128)(2,1)S(1)}, u32[]{:S(2)}, u32[]{:S(2)}) async-start(bf16[8,32,1024]{2,1,0:T(8,128)(2,1)} %copy.35), calls=%async_computation | async-start | bytes 1048576 | tf_op jit(solution)/shard_map/all_to_all | solution.py:115
  113.0 36.5 %all-gather.6.cloned.1.call-start = ((), (), s32[]{:S(2)}) async-start(), calls=%async_computation.4 | async-start | bytes 1310720 | tf_op jit(solution)/shard_map/all_gather | solution.py:123
  123.9 181.0 %all-reduce.6.cloned.1.call-start = ((), (), s32[]{:S(2)}) async-start(), calls=%async_computation.5 | async-start | bytes 2097152 | tf_op jit(solution)/shard_map/psum | solution.py:141
  128.7 3.2 copy-start.7
  152.3 3.8 copy-start.4
  173.0 3.7 copy-start.1
  195.0 3.7 copy-start.1
  216.9 3.7 copy-start.1
  238.9 3.7 copy-start.1
  244.8 1.5 copy-start.2
  247.5 2.4 copy-start.3
  253.4 93.0 %all-gather.8.cloned.1.call-start = ((), (), s32[]{:S(2)}) async-start(), calls=%async_computation.6 | async-start | bytes 1310720 | tf_op jit(solution)/shard_map/all_gather | solution.py:151
  320.9 111.9 %all-reduce.8.cloned.1.call-start = ((), (), s32[]{:S(2)}) async-start(), calls=%async_computation.7 | async-start | bytes 8388608 | tf_op jit(solution)/shard_map/psum | solution.py:157
Sparse Core Ops, SparseCore 0:
  9.9 39.2 all-gather.3
  54.9 51.8 all-reduce.3
  124.0 25.4 all-gather.5
  253.6 51.2 all-reduce.5
  321.0 25.4 all-gather.7
  352.5 80.1 all-reduce.7
where the time goes:
time: 443 us; the launch traced here: 442 us
  waiting for transfers between devices  272 us (61%)
  matrix products  96.6 us (22%)
  other arithmetic  20.8 us (5%)
  local copies, waits for them, and re-layouts  20.3 us (5%)
  between operations  14.3 us (3%)
  blocking collectives  13.2 us (3%)
    psum x1, waiting for transfers between devices, per_device(): lax.psum(weight_part.astype(jnp.bfloat16), 'doc').astype(jnp.float32)  77.2 us
    psum x1, waiting for transfers between devices, per_device(): lax.psum(partial_value.astype(jnp.bfloat16), 'seq').astype(jnp.float32)  51.8 us
    psum x1, waiting for transfers between devices, per_device(): grad_sum = lax.psum(grad_kv.astype(jnp.bfloat16), 'seq').astype(jnp.float32)  51.4 us
    all_gather x1, waiting for transfers between devices, per_device(): lax.all_gather(kv_weight, 'doc', axis=0, tiled=True)  41.2 us
    dot_general x4, matrix products, one_head(): jnp.einsum('tgl,tgd->ld', grad_low, query_head, preferred_element_type=jn...  39.3 us
    all_gather x1, waiting for transfers between devices, per_device(): grad_full = lax.all_gather(returned, 'seq', axis=1, tiled=True)  25.3 us
    all_gather x1, waiting for transfers between devices, per_device(): kv_full = lax.all_gather(kv_part, 'seq', axis=1, tiled=True)  16.2 us
    all_to_all x1, blocking collectives, per_device(): lax.all_to_all(back_out, 'doc', split_axis=0, concat_axis=0, tiled=True)  13.2 us
  transfers between devices with their start and end apart: 7, of which 7 were waited for; matrix products, arithmetic and copies ran while one was open for 3% of the time, Pallas kernels for 0%

commit v1 on v0

--- a/solution.py
+++ b/solution.py
@@ -96,7 +96,9 @@
     own_cols = images[0].reshape(slots * tile_rows, images.shape[3])
     partial_value = lax.dot_general(
         own_cols,
-        lax.all_gather(kv_weight, "doc", axis=0, tiled=True),
+        jnp.concatenate(
+            lax.all_to_all(jnp.stack([kv_weight] * lax.axis_size("doc")), "doc", 0, 0), axis=0
+        ),
         (((1,), (1,)), ((), ())),
         preferred_element_type=jnp.float32,
     )

time: 443 us -> 453 us (1.023)
  blocking collectives: 13.2 us -> 67.2 us
  waiting for transfers between devices: 272 us -> 230 us
    all_to_all x0 -> x1, blocking collectives: none -> 54 us  [per_device(): lax.all_to_all(jnp.stack([kv_weight] * lax.axis_size('doc')), 'doc', 0, 0)]
    all_gather x1 -> x0, waiting for transfers between devices: 41.2 us -> none  [per_device(): lax.all_gather(kv_weight, 'doc', axis=0, tiled=True)]
  transfers between devices with their start and end apart: 7 -> 6, of which waited for: 7 -> 6; matrix products, arithmetic and copies ran while one was open for 3% -> 3% of each run, Pallas kernels for 0% -> 0%
where the time goes in v1:
time: 453 us; the launch traced here: 452 us
  waiting for transfers between devices  230 us (51%)
  matrix products  94.5 us (21%)
  blocking collectives  67.2 us (15%)
  local copies, waits for them, and re-layouts  21.9 us (5%)
  other arithmetic  20.7 us (5%)
  between operations  14 us (3%)
    psum x1, waiting for transfers between devices, per_device(): lax.psum(weight_part.astype(jnp.bfloat16), 'doc').astype(jnp.float32)  77.2 us
    all_to_all x1, blocking collectives, per_device(): lax.all_to_all(jnp.stack([kv_weight] * lax.axis_size('doc')), 'doc', 0, 0)  54 us
    psum x1, waiting for transfers between devices, per_device(): grad_sum = lax.psum(grad_kv.astype(jnp.bfloat16), 'seq').astype(jnp.float32)  51.4 us
    psum x1, waiting for transfers between devices, per_device(): lax.psum(partial_value.astype(jnp.bfloat16), 'seq').astype(jnp.float32)  51.2 us
    dot_general x4, matrix products, one_head(): jnp.einsum('tgl,tgd->ld', grad_low, query_head, preferred_element_type=jn...  39.3 us
    all_gather x1, waiting for transfers between devices, per_device(): grad_full = lax.all_gather(returned, 'seq', axis=1, tiled=True)  25.3 us
    all_gather x1, waiting for transfers between devices, per_device(): kv_full = lax.all_gather(kv_part, 'seq', axis=1, tiled=True)  16.1 us
    all_to_all x1, blocking collectives, per_device(): lax.all_to_all(back_out, 'doc', split_axis=0, concat_axis=0, tiled=True)  13.2 us
  transfers between devices with their start and end apart: 6, of which 6 were waited for; matrix products, arithmetic and copies ran while one was open for 3% of the time, Pallas kernels for 0%

profile of v1, /device:TPU:0, one launch (start us, length us, event | category | flops | bytes accessed | tf_op | source)
XLA Modules:
  0.0 452.3 jit_solution(15733421726068148780)
XLA Ops:
  7.2 1.7 stack.2
  8.9 54.0 %all_to_all.15 = bf16[8,128,2048]{2,1,0:T(8,128)(2,1)S(1)} all-to-all(bf16[8,128,2048]{2,1,0:T(8,128)(2,1)S(1)} %stack.2), channel_id=1, replica_groups=mesh['doc'=8,'seq'=4] {'doc'}, dimensions={0} | all-to-all | bytes 8388608 | tf_op jit(solution)/shard_map/all_to_all | solution.py:100
  63.0 3.3 fusion.63
  66.5 51.2 %all-reduce.4.cloned.1.call-done = bf16[4,128,1024]{2,1,0:T(8,128)(2,1)} async-done(((bf16[4,128,1024]{2,1,0:T(8,128)(2,1)}), bf16[4,128,1024]{2,1,0:T(8,128)(2,1)}) %all-reduce.4.cloned.1.call-update) | async-done | bytes 1048592 | tf_op jit(solution)/shard_map/psum | solution.py:107
  120.3 3.7 all-to-all-start.1
  125.3 8.4 %all-to-all-done.1 = bf16[8,32,1024]{2,1,0:T(8,128)(2,1)S(1)} async-done(((bf16[8,32,1024]{2,1,0:T(8,128)(2,1)}), bf16[8,32,1024]{2,1,0:T(8,128)(2,1)S(1)}, u32[]{:S(2)}, u32[]{:S(2)}) %all-to-all-start.1) | async-done | bytes 524320 | tf_op jit(solution)/shard_map/all_to_all | solution.py:117
  135.7 2.3 copy.40
  138.0 1.6 copy.33
  140.6 2.3 multiply_bitcast_fusion
  142.9 1.4 fusion.66
  144.3 16.1 %all-gather.3.cloned.1.call-done = bf16[4,128,1024]{2,0,1:T(4,128)(2,1)} async-done(((bf16[4,32,1024]{2,0,1:T(4,128)(2,1)}), bf16[4,128,1024]{2,0,1:T(4,128)(2,1)}) %all-gather.3.cloned.1.call-update) | async-done | bytes 1048592 | tf_op jit(solution)/shard_map/all_gather | solution.py:125
  160.4 1.5 copy.37
  161.9 1.3 fusion.86
  163.3 1.6 copy.38
  165.0 2.1 copy.39
  168.0 87.8 %while.15 = (s32[]{:T(128)}, bf16[4,128,8,128]{3,1,2,0:T(8,128)(2,1)}, f32[4,512,128]{1,2,0:T(8,128)}, bf16[4,512,128]{2,1,0:T(8,128)(2,1)}, bf16[4,128,8,128]{1...) while((s32[]{:T(128)}, ...), condition=%wide.region_6.7_spmd.clone, body=%wide.region_3.6_spmd.clone.sunk | while | flops 682891136 | bytes 27433116 | solution.py:62
  168.5 2.8 fusion.113
  171.3 2.7 fusion.115
  174.1 9.8 %fusion.116 = f32[4,512,128]{1,2,0:T(8,128)} fusion(f32[4,512,128]{1,2,0:T(8,128)} %get-tuple-element.222, s32[]{:T(128)} %get-tuple-element.220, f32[128,8,512]{2,0,1:T(8,128)} %fusion.115, bf16[4,128,8,128]{1,3,2,0:T(8,128)(2,1)} %get-tuple-element.236, f32[128,8,512]{2,0,1:T(8,128)} %get-tuple-element.206, f32[128,8]{0,1:T(8,128)S(1)} %get-tuple-element.207, ...), kind=kOutput, calls=%fused_computation.13.clone.1 | convolution fusion | flops 139986432 | bytes 8926208 | tf_op jit(solution)/shard_map/while/body/eval_jaxpr/tgl,tgd->ld/dot_general | solution.py:48
  183.9 3.1 fusion.117
  187.7 2.2 fusion.114
  190.5 2.8 fusion.113
  193.3 2.7 fusion.115
  196.0 9.8 %fusion.116 = f32[4,512,128]{1,2,0:T(8,128)} fusion(f32[4,512,128]{1,2,0:T(8,128)} %get-tuple-element.222, s32[]{:T(128)} %get-tuple-element.220, f32[128,8,512]{2,0,1:T(8,128)} %fusion.115, bf16[4,128,8,128]{1,3,2,0:T(8,128)(2,1)} %get-tuple-element.236, f32[128,8,512]{2,0,1:T(8,128)} %get-tuple-element.206, f32[128,8]{0,1:T(8,128)S(1)} %get-tuple-element.207, ...), kind=kOutput, calls=%fused_computation.13.clone.1 | convolution fusion | flops 139986432 | bytes 8926208 | tf_op jit(solution)/shard_map/while/body/eval_jaxpr/tgl,tgd->ld/dot_general | solution.py:48
  205.8 3.1 fusion.117
  209.6 2.2 fusion.114
  212.4 2.8 fusion.113
  215.2 2.7 fusion.115
  218.0 9.8 %fusion.116 = f32[4,512,128]{1,2,0:T(8,128)} fusion(f32[4,512,128]{1,2,0:T(8,128)} %get-tuple-element.222, s32[]{:T(128)} %get-tuple-element.220, f32[128,8,512]{2,0,1:T(8,128)} %fusion.115, bf16[4,128,8,128]{1,3,2,0:T(8,128)(2,1)} %get-tuple-element.236, f32[128,8,512]{2,0,1:T(8,128)} %get-tuple-element.206, f32[128,8]{0,1:T(8,128)S(1)} %get-tuple-element.207, ...), kind=kOutput, calls=%fused_computation.13.clone.1 | convolution fusion | flops 139986432 | bytes 8926208 | tf_op jit(solution)/shard_map/while/body/eval_jaxpr/tgl,tgd->ld/dot_general | solution.py:48
  227.8 3.1 fusion.117
  231.6 2.2 fusion.114
  234.4 2.8 fusion.113
  237.2 2.7 fusion.115
  239.9 9.8 %fusion.116 = f32[4,512,128]{1,2,0:T(8,128)} fusion(f32[4,512,128]{1,2,0:T(8,128)} %get-tuple-element.222, s32[]{:T(128)} %get-tuple-element.220, f32[128,8,512]{2,0,1:T(8,128)} %fusion.115, bf16[4,128,8,128]{1,3,2,0:T(8,128)(2,1)} %get-tuple-element.236, f32[128,8,512]{2,0,1:T(8,128)} %get-tuple-element.206, f32[128,8]{0,1:T(8,128)S(1)} %get-tuple-element.207, ...), kind=kOutput, calls=%fused_computation.13.clone.1 | convolution fusion | flops 139986432 | bytes 8926208 | tf_op jit(solution)/shard_map/while/body/eval_jaxpr/tgl,tgd->ld/dot_general | solution.py:48
  249.7 3.1 fusion.117
  253.5 2.2 fusion.114
  255.8 1.5 fusion.69
  261.8 2.5 pad_maximum_fusion
  264.4 51.4 %all-reduce.6.cloned.1.call-done = bf16[4,128,1024]{2,0,1:T(4,128)(2,1)} async-done(((bf16[4,128,1024]{2,0,1:T(4,128)(2,1)}), bf16[4,128,1024]{2,0,1:T(4,128)(2,1)}) %all-reduce.6.cloned.1.call-update) | async-done | bytes 1048592 | tf_op jit(solution)/shard_map/psum | solution.py:143
  315.8 1.4 convolution_convert_fusion.1
  317.4 13.2 %all_to_all.16 = bf16[8,32,1024]{2,1,0:T(8,128)(2,1)S(1)} all-to-all(bf16[8,32,1024]{2,1,0:T(8,128)(2,1)S(1)} %copy.51), channel_id=1, replica_groups=mesh['doc'=8,'seq'=4] {'doc'}, dimensions={0} | all-to-all | bytes 1048576 | tf_op jit(solution)/shard_map/all_to_all | solution.py:149
  332.0 25.3 %all-gather.5.cloned.1.call-done = bf16[4,128,1024]{2,0,1:T(4,128)(2,1)} async-done(((bf16[4,32,1024]{2,0,1:T(4,128)(2,1)}), bf16[4,128,1024]{2,0,1:T(4,128)(2,1)}) %all-gather.5.cloned.1.call-update) | async-done | bytes 1048592 | tf_op jit(solution)/shard_map/all_gather | solution.py:153
  357.4 1.5 copy.53
  358.9 4.3 convolution_convert_fusion
  363.3 1.9 copy.45
  365.2 1.3 broadcast_in_dim_reshape.3
  366.5 77.2 %all-reduce.8.cloned.1.call-done = bf16[1024,2048]{1,0:T(8,128)(2,1)} async-done(((bf16[1024,2048]{1,0:T(8,128)(2,1)}), bf16[1024,2048]{1,0:T(8,128)(2,1)}) %all-reduce.8.cloned.1.call-update) | async-done | bytes 4194320 | tf_op jit(solution)/shard_map/psum | solution.py:159
  443.6 2.1 dynamic-slice_convert_fusion
  (71 shorter events, 19.4 us)
Async XLA Ops:
  7.2 55.8 %copy-start = (bf16[1,4,128,2048]{3,2,1,0:T(8,128)(2,1)S(1)}, bf16[1,4,128,2048]{3,2,1,0:T(8,128)(2,1)}, u32[]{:S(2)}) copy-start(bf16[1,4,128,2048]{3,2,1,0:T(8,128)(2,1)} %param.12) | copy-start | bytes 6291460
  7.2 110.6 %all-reduce.4.cloned.1.call-start = ((), (), s32[]{:S(2)}) async-start(), calls=%async_computation.3 | async-start | bytes 2097152 | tf_op jit(solution)/shard_map/psum | solution.py:107
  63.0 3.4 copy-start.5
  66.3 57.7 %copy-start.8 = (s32[8]{0:T(128)S(1)}, s32[8]{0:T(128)}, u32[]{:S(2)}) copy-start(s32[8]{0:T(128)} %param.18) | copy-start | bytes 100
  66.3 58.2 %copy-start.6 = (s32[8,4]{0,1:T(4,128)S(1)}, s32[8,4]{0,1:T(4,128)}, u32[]{:S(2)}) copy-start(s32[8,4]{0,1:T(4,128)} %param.20) | copy-start | bytes 388
  118.7 16.3 %copy-start.9 = (s32[8]{0:T(128)S(1)}, s32[8]{0:T(128)}, u32[]{:S(2)}) copy-start(s32[8]{0:T(128)} %param.21) | copy-start | bytes 100
  120.3 13.4 %all-to-all-start.1 = ((bf16[8,32,1024]{2,1,0:T(8,128)(2,1)}), bf16[8,32,1024]{2,1,0:T(8,128)(2,1)S(1)}, u32[]{:S(2)}, u32[]{:S(2)}) async-start(bf16[8,32,1024]{2,1,0:T(8,128)(2,1)} %copy.35), calls=%async_computation.1 | async-start | bytes 1048576 | tf_op jit(solution)/shard_map/all_to_all | solution.py:117
  123.9 36.5 %all-gather.3.cloned.1.call-start = ((), (), s32[]{:S(2)}) async-start(), calls=%async_computation.4 | async-start | bytes 1310720 | tf_op jit(solution)/shard_map/all_gather | solution.py:125
  134.8 181.0 %all-reduce.6.cloned.1.call-start = ((), (), s32[]{:S(2)}) async-start(), calls=%async_computation.5 | async-start | bytes 2097152 | tf_op jit(solution)/shard_map/psum | solution.py:143
  139.6 3.2 copy-start.7
  163.3 3.8 copy-start.4
  183.9 3.8 copy-start.1
  205.8 3.8 copy-start.1
  227.8 3.8 copy-start.1
  249.7 3.8 copy-start.1
  255.8 1.5 copy-start.2
  258.4 2.4 copy-start.3
  264.4 93.0 %all-gather.5.cloned.1.call-start = ((), (), s32[]{:S(2)}) async-start(), calls=%async_computation.6 | async-start | bytes 1310720 | tf_op jit(solution)/shard_map/all_gather | solution.py:153
  331.8 111.8 %all-reduce.8.cloned.1.call-start = ((), (), s32[]{:S(2)}) async-start(), calls=%async_computation.7 | async-start | bytes 8388608 | tf_op jit(solution)/shard_map/psum | solution.py:159
Sparse Core Ops, SparseCore 0:
  66.5 51.2 all-reduce.3
  134.9 25.4 all-gather.2
  264.5 51.2 all-reduce.5
  331.9 25.4 all-gather.4
  363.4 80.1 all-reduce.7
